TPU v7x, 128 devices: a whole 4x4x4 slice. The times are simulated.
128 devices in a mesh: rep: 8 (over z, core), tab: 16 (over x, y).
Axes of the slice: x: 4, y: 4, z: 4, core: 2. Of those that a mesh axis runs over, the one named last changes fastest.
Arguments:
- inputs: bfloat16 [16384, 4096], P(('rep', 'tab')), may hold values from -24 to 24
- grad_out: bfloat16 [16384, 4096], P(('rep', 'tab')), may hold values from -6 to 6
- query_weight: bfloat16 [4096, 1024], replicated, may hold values from -0.09375 to 0.09375
- sub_keys: bfloat16 [1024, 1024], replicated, may hold values from -6 to 6
- values: bfloat16 [4096, 4096], P('tab'), may hold values from -0.09375 to 0.09375
- owner: int32 [16384, 2, 1], P(('rep', 'tab')), may hold values from 0 to 15; in each aligned block of 256 rows (0 to 255, 256 to 511, ..., all dimensions but the last counted through in order) at most 32 rows name the same one
- slot_rows: int32 [16384, 2, 32], P(('rep', 'tab')), may hold values from 0 to 255, as said below
- sub_index: int32 [16384, 2, 2, 32], P(('rep', 'tab')), may hold values from 0 to 1023
Outputs:
- input_grad: bfloat16 [16384, 4096], P(('rep', 'tab'))
- weight_grad: float32 [4096, 1024], P('tab')
- key_grad: float32 [1024, 1024], P('tab')
- table_grad: bfloat16 [4096, 4096], P('tab')
Inputs may be any that keep to these rules, and one draw needn't show every extreme that they name: `owner`: within the token-head pairs of one device (aligned blocks of 256 pairs), no shard number appears more than 32 times, and one appears exactly 32 times in some or all blocks. `slot_rows`: the 32 row numbers of one token and head are distinct.
All inputs are finite; a program needn't handle non-finite values.
Results may differ from a plain program's by a relative error of at most 0.0059.
Values may be sent and summed in bfloat16 or wider, within the bound.
A program may use at most 192 MiB of HBM per device.

v0:
```python
import math
import jax
import jax.numpy as jnp
from jax import lax
from jax.sharding import PartitionSpec as P


def weight_term(input_blocks, query_grad):
    return jnp.einsum("tgd,tk->gdk", input_blocks, query_grad, preferred_element_type=jnp.float32)


def key_term(grad_blocks, query_blocks, many, width):
    key_part = jnp.einsum(
        "tbgs,tbc->gsbc", grad_blocks, query_blocks, preferred_element_type=jnp.float32
    )
    return key_part.reshape(many, key_part.shape[1], width)


def grad_term(input_blocks, grad_blocks, query_grad, query_blocks, many):
    weight_part = weight_term(input_blocks, query_grad)
    key_part = key_term(grad_blocks, query_blocks, many, weight_part.shape[2])
    joined = jnp.concatenate([weight_part, key_part], axis=1)
    return joined.reshape(many * joined.shape[1], weight_part.shape[2])


def on_device(inputs, grad_out, query_weight, sub_keys, values, owner, slot_rows, sub_index):
    tokens = inputs.shape[0]
    model_width = inputs.shape[1]
    query_cols = query_weight.shape[1]
    key_count = sub_keys.shape[0]
    head_count = slot_rows.shape[1]
    top_count = slot_rows.shape[2]
    blocks = 2 * head_count
    half_width = query_cols // blocks
    shards = lax.axis_size("tab")
    table_rows = values.shape[0]
    capacity = 2 * tokens * head_count // shards
    messages = tokens * head_count
    slots = shards * capacity
    block_tokens = math.gcd(tokens, 64)
    block_count = tokens // block_tokens
    key_iota = jnp.arange(key_count, dtype=jnp.int32)
    query = jnp.dot(inputs, query_weight, preferred_element_type=jnp.float32)
    low_query = query.astype(jnp.bfloat16)
    query_blocks = low_query.reshape(tokens, blocks, half_width)
    key_blocks = sub_keys.reshape(key_count, blocks, half_width)
    key_wide = sub_keys.astype(jnp.float32).reshape(key_count, blocks, half_width)
    half_scores = jnp.einsum(
        "tbc,nbc->tbn",
        query.reshape(tokens, blocks, half_width),
        key_wide,
        precision=lax.Precision.HIGHEST,
    )
    picks = sub_index.reshape(tokens, blocks, top_count)

    def pick_block(pair):
        block_scores, block_picks = pair
        equal = block_picks[:, :, :, None] == key_iota[None, None, None, :]
        return jnp.sum(jnp.where(equal, block_scores[:, :, None, :], 0.0), axis=3)

    chosen = lax.map(
        pick_block,
        (
            half_scores.reshape(block_count, block_tokens, blocks, key_count),
            picks.reshape(block_count, block_tokens, blocks, top_count),
        ),
    )
    chosen = chosen.reshape(tokens, head_count, 2, top_count)
    scores = chosen[:, :, 0] + chosen[:, :, 1]
    weights = jax.nn.softmax(scores, axis=-1)
    low_weights = weights.astype(jnp.bfloat16)
    target = owner.reshape(messages)
    onehot = (target[:, None] == jnp.arange(shards, dtype=jnp.int32)[None, :]).astype(jnp.float32)
    message_iota = jnp.arange(messages, dtype=jnp.int32)
    lower = (message_iota[:, None] > message_iota[None, :]).astype(jnp.float32)
    before = jnp.dot(lower, onehot, precision=lax.Precision.HIGHEST)
    position = jnp.sum(before * onehot, axis=1).astype(jnp.int32)
    slot_of = target * capacity + position
    dispatch = jnp.arange(slots, dtype=jnp.int32)[:, None] == slot_of[None, :]
    token_dispatch = jnp.any(dispatch.reshape(slots, tokens, head_count), axis=2).astype(
        jnp.bfloat16
    )
    payload = jnp.dot(token_dispatch, grad_out, preferred_element_type=jnp.float32).astype(
        jnp.bfloat16
    )
    dispatch_wide = dispatch.astype(jnp.float32)
    send_rows = jnp.dot(
        dispatch_wide,
        slot_rows.reshape(messages, top_count).astype(jnp.float32),
        precision=lax.Precision.HIGHEST,
    ).astype(jnp.int32)
    send_weights = jnp.dot(
        dispatch.astype(jnp.bfloat16),
        low_weights.reshape(messages, top_count),
        preferred_element_type=jnp.float32,
    ).astype(jnp.bfloat16)
    arrived, arrived_index, arrived_weights = (
        lax.all_to_all(
            payload.reshape(shards, capacity, model_width),
            "tab",
            split_axis=0,
            concat_axis=0,
            tiled=True,
        ),
        lax.all_to_all(
            send_rows.reshape(shards, capacity, top_count),
            "tab",
            split_axis=0,
            concat_axis=0,
            tiled=True,
        ),
        lax.all_to_all(
            send_weights.reshape(shards, capacity, top_count),
            "tab",
            split_axis=0,
            concat_axis=0,
            tiled=True,
        ),
    )
    arrived = arrived.reshape(slots, model_width)
    arrived_index = arrived_index.reshape(slots, top_count)
    arrived_weights = arrived_weights.reshape(slots, top_count)
    products = lax.dot_general(
        arrived, values, (((1,), (1,)), ((), ())), preferred_element_type=jnp.float32
    )
    table_iota = jnp.arange(table_rows, dtype=jnp.int32)
    matches = arrived_index[:, :, None] == table_iota[None, None, :]
    slot_back = jnp.sum(jnp.where(matches, products[:, None, :], 0.0), axis=2)
    spread_table = jnp.sum(
        jnp.where(matches, arrived_weights[:, :, None].astype(jnp.float32), 0.0), axis=1
    ).astype(jnp.bfloat16)
    table_part = lax.dot_general(
        spread_table, arrived, (((0,), (0,)), ((), ())), preferred_element_type=jnp.float32
    )
    returned = lax.all_to_all(
        slot_back.reshape(shards, capacity, top_count),
        "tab",
        split_axis=0,
        concat_axis=0,
        tiled=True,
    )
    slot_grad = lax.dot_general(
        dispatch_wide,
        returned.reshape(slots, top_count),
        (((0,), (0,)), ((), ())),
        precision=lax.Precision.HIGHEST,
    ).reshape(tokens, head_count, top_count)
    score_grad = weights * (slot_grad - jnp.sum(weights * slot_grad, axis=-1, keepdims=True))
    spread_grad = jnp.broadcast_to(
        score_grad[:, :, None, :], (tokens, head_count, 2, top_count)
    ).reshape(tokens, blocks, top_count)

    def place_block(pair):
        block_spread, block_picks = pair
        equal = block_picks[:, :, :, None] == key_iota[None, None, None, :]
        return jnp.sum(jnp.where(equal, block_spread[:, :, :, None], 0.0), axis=2)

    half_grad = lax.map(
        place_block,
        (
            spread_grad.reshape(block_count, block_tokens, blocks, top_count),
            picks.reshape(block_count, block_tokens, blocks, top_count),
        ),
    )
    half_grad = half_grad.reshape(tokens, blocks, key_count).astype(jnp.bfloat16)
    query_grad = (
        jnp.einsum("tbn,nbc->tbc", half_grad, key_blocks, preferred_element_type=jnp.float32)
        .astype(jnp.bfloat16)
        .reshape(tokens, query_cols)
    )
    input_grad = lax.dot_general(
        query_grad, query_weight, (((1,), (1,)), ((), ())), preferred_element_type=jnp.float32
    ).astype(jnp.bfloat16)
    weight_rows = model_width // shards
    key_rows = key_count // shards
    per_device = weight_rows + key_rows
    input_blocks = inputs.reshape(tokens, shards, weight_rows)
    grad_blocks = half_grad.reshape(tokens, blocks, shards, key_rows)
    local = lax.psum_scatter(
        grad_term(
            input_blocks,
            grad_blocks,
            query_grad,
            query_blocks,
            per_device * lax.axis_size("tab") // per_device,
        ),
        "tab",
        scatter_dimension=0,
        tiled=True,
    )
    local_sum, table_sum = lax.psum((local, table_part), "rep")
    weight_grad = local_sum[:weight_rows]
    key_grad = local_sum[weight_rows:]
    return (input_grad, weight_grad, key_grad, table_sum.astype(jnp.bfloat16))


def solution(mesh):
    placed = (
        P(("rep", "tab"), None),
        P(("rep", "tab"), None),
        P(),
        P(),
        P("tab", None),
        P(("rep", "tab"), None, None),
        P(("rep", "tab"), None, None),
        P(("rep", "tab"), None, None, None),
    )
    return jax.shard_map(
        on_device,
        mesh=mesh,
        in_specs=placed,
        out_specs=(P(("rep", "tab"), None), P("tab", None), P("tab", None), P("tab", None)),
        check_vma=False,
    )
```

profile of v0, /device:TPU:0, one launch (start us, length us, event | category | flops | bytes accessed | tf_op | source)
XLA Modules:
  0.0 426.2 jit_solution(7707619019839026984)
XLA Ops:
  8.4 5.8 %fusion.36 = (bf16[128,1024]{1,0:T(8,128)(2,1)}, f32[128,1024]{1,0:T(8,128)S(1)}) fusion(bf16[128,4096]{1,0:T(8,128)(2,1)} %param.12, bf16[4096,1024]{1,0:T(8,128)(2,1)} %param.14), kind=kOutput, calls=%fused_computation.62 | convolution fusion | flops 1073872896 | bytes 10223616 | tf_op jit(solution)/shard_map/dot_general | solution.py:43
  14.2 3.5 fusion.6
  17.7 16.5 %while.22 = (s32[]{:T(128)}, f32[2,64,4,32]{3,2,1,0:T(4,128)}, s32[2,64,4,32]{3,2,1,0:T(4,128)S(1)}, f32[2,64,4,1024]{3,1,0,2:T(8,128)}, s32[]{:T(128)}) while((s32[]{:T(128)}, f32[2,64,4,32]{3,2,1,0:T(4,128)}, s32[2,64,4,32]{3,2,1,0:T(4,128)S(1)}, f32[2,64,4,1024]{3,1,0,2:T(8,128)}, s32[]{:T(128)}) %tuple.62), condition=%wide.region_2.3_spmd.clone, body=%wide.region_0.2_spmd.clone.sunk | while | flops 25157632 | bytes 5538373 | solution.py:61
  19.7 5.5 %select_reduce_fusion.6 = f32[64,4,32]{2,1,0:T(4,128)S(1)} fusion(f32[64,4,1024]{2,1,0:T(4,128)S(1)} %bitcast.121, s32[64,4,32]{2,1,0:T(4,128)S(1)} %dynamic-slice_bitcast_fusion.6), kind=kLoop, calls=%fused_computation.3.clone.1 | loop fusion | flops 25157632 | bytes 1114112 | tf_op jit(solution)/shard_map/while/body/eval_jaxpr/reduce_sum | solution.py:59
  27.9 5.5 %select_reduce_fusion.6 = f32[64,4,32]{2,1,0:T(4,128)S(1)} fusion(f32[64,4,1024]{2,1,0:T(4,128)S(1)} %bitcast.121, s32[64,4,32]{2,1,0:T(4,128)S(1)} %dynamic-slice_bitcast_fusion.6), kind=kLoop, calls=%fused_computation.3.clone.1 | loop fusion | flops 25157632 | bytes 1114112 | tf_op jit(solution)/shard_map/while/body/eval_jaxpr/reduce_sum | solution.py:59
  48.8 7.1 %all-to-all-start.3 = ((bf16[16,2,512]{2,1,0:T(2,128)(2,1)}), bf16[16,2,512]{2,1,0:T(2,128)(2,1)S(1)}, u32[]{:S(2)}, u32[]{:S(2)}) async-start(bf16[16,2,512]{2,1,0:T(2,128)(2,1)} %reshape.169), calls=%async_computation.4 | async-start | bytes 65536 | tf_op jit(solution)/shard_map/all_to_all | solution.py:112
  69.8 7.3 %all-to-all-start = ((s32[16,1,1024]{2,1,0:T(1,128)}), s32[16,1,1024]{2,1,0:T(1,128)}, u32[]{:S(2)}, u32[]{:S(2)}) async-start(s32[16,1,1024]{2,1,0:T(1,128)} %reshape.171), calls=%async_computation | async-start | bytes 131072 | tf_op jit(solution)/shard_map/all_to_all | solution.py:105
  77.1 3.2 convolution_convert_fusion
  80.3 4.5 %all-to-all-done = s32[16,1,1024]{2,1,0:T(1,128)} async-done(((s32[16,1,1024]{2,1,0:T(1,128)}), s32[16,1,1024]{2,1,0:T(1,128)}, u32[]{:S(2)}, u32[]{:S(2)}) %all-to-all-start) | async-done | bytes 65568 | tf_op jit(solution)/shard_map/all_to_all | solution.py:105
  84.8 4.5 %all-to-all-start.1 = ((bf16[16,32,4096]{2,1,0:T(8,128)(2,1)}), bf16[16,32,4096]{2,1,0:T(8,128)(2,1)}, u32[]{:S(2)}, u32[]{:S(2)}) async-start(bf16[16,32,4096]{2,1,0:T(8,128)(2,1)} %bitcast.123), calls=%async_computation.1 | async-start | bytes 8388608 | tf_op jit(solution)/shard_map/all_to_all | solution.py:98
  93.4 49.6 %all-to-all-done.1 = bf16[16,32,4096]{2,1,0:T(8,128)(2,1)} async-done(((bf16[16,32,4096]{2,1,0:T(8,128)(2,1)}), bf16[16,32,4096]{2,1,0:T(8,128)(2,1)}, u32[]{:S(2)}, u32[]{:S(2)}) %all-to-all-start.1) | async-done | bytes 4194336 | tf_op jit(solution)/shard_map/all_to_all | solution.py:98
  143.1 3.6 fusion.37
  146.6 10.9 %select_reduce_fusion.2 = (bf16[512,256]{1,0:T(8,128)(2,1)}, f32[512,32]{1,0:T(8,128)S(1)}) fusion(f32[512,32]{1,0:T(8,128)} %bitcast.142, s32[512,32]{1,0:T(8,128)S(1)} %bitcast.143, f32[512,256]{1,0:T(8,128)S(1)} %fusion.37), kind=kLoop, calls=%fused_computation.14 | loop fusion | flops 20824064 | bytes 983040 | tf_op jit(solution)/shard_map/reduce_sum | solution.py:129
  158.5 3.8 all-to-all-start.2
  164.2 5.8 %all-to-all-done.2 = f32[16,1,1024]{2,1,0:T(1,128)S(1)} async-done(((f32[16,1,1024]{2,1,0:T(1,128)}), f32[16,1,1024]{2,1,0:T(1,128)S(1)}, u32[]{:S(2)}, u32[]{:S(2)}) %all-to-all-start.2) | async-done | bytes 65568 | tf_op jit(solution)/shard_map/all_to_all | solution.py:135
  172.3 17.1 %while.23 = (s32[]{:T(128)}, bf16[2,64,4,1024]{3,2,1,0:T(4,128)(2,1)S(1)}, s32[2,64,4,32]{3,2,1,0:T(4,128)S(1)}, f32[2,64,4,32]{3,2,1,0:T(4,128)S(1)}, s32[]{:T(128)}) while((s32[]{:T(128)}, bf16[2,64,4,1024]{3,2,1,0:T(4,128)(2,1)S(1)}, s32[2,64,4,32]{3,2,1,0:T(4,128)S(1)}, f32[2,64,4,32]{3,2,1,0:T(4,128)S(1)}, s32[]{:T(128)}) %tuple.64), condition=%wide.region_11.12_spmd.clone, body=%wide.region_9.11_spmd.clone.sunk | while | flops 24903680 | bytes 1769545 | solution.py:158
  172.4 8.3 %select_reduce_fusion.7 = bf16[64,4,1024]{2,1,0:T(4,128)(2,1)S(1)} fusion(f32[64,4,32]{2,1,0:T(4,128)S(1)} %dynamic-slice_bitcast_fusion.7, s32[64,4,32]{2,1,0:T(4,128)S(1)} %dynamic-slice_bitcast_fusion.8), kind=kLoop, calls=%fused_computation.9.clone.1 | loop fusion | flops 24903680 | bytes 589824 | tf_op jit(solution)/shard_map/while/body/eval_jaxpr/reduce_sum | solution.py:156
  181.0 8.3 %select_reduce_fusion.7 = bf16[64,4,1024]{2,1,0:T(4,128)(2,1)S(1)} fusion(f32[64,4,32]{2,1,0:T(4,128)S(1)} %dynamic-slice_bitcast_fusion.7, s32[64,4,32]{2,1,0:T(4,128)S(1)} %dynamic-slice_bitcast_fusion.8), kind=kLoop, calls=%fused_computation.9.clone.1 | loop fusion | flops 24903680 | bytes 589824 | tf_op jit(solution)/shard_map/while/body/eval_jaxpr/reduce_sum | solution.py:156
  190.4 3.1 reshape.168
  203.7 9.2 %pad_maximum_fusion = f32[16,320,1024]{2,1,0:T(8,128)} fusion(f32[16,64,1024]{2,1,0:T(8,128)S(1)} %bitcast.125, f32[16,256,1024]{2,1,0:T(8,128)S(1)} %convolution_bitcast_fusion), kind=kLoop, calls=%fused_computation.13 | loop fusion | flops 5242880 | bytes 41943040 | tf_op jit(solution)/shard_map/concatenate | solution.py:22
  213.8 5.4 %fusion.38 = f32[256,4096]{1,0:T(8,128)} fusion(bf16[512,256]{1,0:T(8,128)(2,1)S(1)} %copy-done.5, bf16[512,4096]{1,0:T(8,128)(2,1)} %bitcast.9), kind=kOutput, calls=%fused_computation.66 | convolution fusion | flops 1073741824 | bytes 8650752 | tf_op jit(solution)/shard_map/dot_general | solution.py:132
  219.3 124.3 %reduce-scatter.2.cloned.1.call-done = f32[320,1024]{1,0:T(8,128)} async-done(((f32[5120,1024]{1,0:T(8,128)}), f32[320,1024]{1,0:T(8,128)}) %reduce-scatter.2.cloned.1.call-update) | async-done | bytes 1310736 | tf_op jit(solution)/shard_map/reduce_scatter | solution.py:179
  343.6 64.3 %all-reduce.4 = bf16[256,4096]{1,0:T(8,128)(2,1)} all-reduce(f32[256,4096]{1,0:T(8,128)} %fusion.38), channel_id=1, replica_groups=mesh['rep'=8,'tab'=16] {'rep'}, use_global_device_ids=true, to_apply=%region_15.16 | all-reduce | flops 1048576 | bytes 6291456 | tf_op jit(solution)/shard_map/psum | solution.py:191
  407.9 7.4 %convolution_convert_fusion.1 = bf16[128,4096]{1,0:T(8,128)(2,1)} fusion(bf16[128,1024]{0,1:T(8,128)(2,1)S(1)} %bitcast.132, bf16[4096,1024]{1,0:T(8,128)(2,1)} %param.14), kind=kOutput, calls=%fused_computation.19 | convolution fusion | flops 1074266112 | bytes 9699328 | tf_op jit(solution)/shard_map/dot_general | solution.py:171
  (102 shorter events, 60.6 us)
Async XLA Ops:
  7.2 135.9 %copy-start = (bf16[256,4096]{1,0:T(8,128)(2,1)S(1)}, bf16[256,4096]{1,0:T(8,128)(2,1)}, u32[]{:S(2)}) copy-start(bf16[256,4096]{1,0:T(8,128)(2,1)} %param.16) | copy-start | bytes 6291460
  8.4 5.8 %copy-start.4 = (bf16[1024,1024]{1,0:T(8,128)(2,1)S(1)}, bf16[1024,1024]{1,0:T(8,128)(2,1)}, u32[]{:S(2)}) copy-start(bf16[1024,1024]{1,0:T(8,128)(2,1)} %param.15) | copy-start | bytes 6291460
  17.7 24.9 %copy-start.10 = (s32[128,2,1]{0,2,1:T(1,128)S(1)}, s32[128,2,1]{0,2,1:T(1,128)}, u32[]{:S(2)}) copy-start(s32[128,2,1]{0,2,1:T(1,128)} %param.17) | copy-start | bytes 3076
  34.2 42.9 %copy-start.6 = (bf16[128,4096]{1,0:T(8,128)(2,1)S(1)}, bf16[128,4096]{1,0:T(8,128)(2,1)}, u32[]{:S(2)}) copy-start(bf16[128,4096]{1,0:T(8,128)(2,1)} %param.13) | copy-start | bytes 3145732
  43.0 0.6 copy-start.9
  48.8 21.0 %all-to-all-start.3 = ((bf16[16,2,512]{2,1,0:T(2,128)(2,1)}), bf16[16,2,512]{2,1,0:T(2,128)(2,1)S(1)}, u32[]{:S(2)}, u32[]{:S(2)}) async-start(bf16[16,2,512]{2,1,0:T(2,128)(2,1)} %reshape.169), calls=%async_computation.4 | async-start | bytes 65536 | tf_op jit(solution)/shard_map/all_to_all | solution.py:112
  69.8 15.0 %all-to-all-start = ((s32[16,1,1024]{2,1,0:T(1,128)}), s32[16,1,1024]{2,1,0:T(1,128)}, u32[]{:S(2)}, u32[]{:S(2)}) async-start(s32[16,1,1024]{2,1,0:T(1,128)} %reshape.171), calls=%async_computation | async-start | bytes 131072 | tf_op jit(solution)/shard_map/all_to_all | solution.py:105
  84.8 58.2 %all-to-all-start.1 = ((bf16[16,32,4096]{2,1,0:T(8,128)(2,1)}), bf16[16,32,4096]{2,1,0:T(8,128)(2,1)}, u32[]{:S(2)}, u32[]{:S(2)}) async-start(bf16[16,32,4096]{2,1,0:T(8,128)(2,1)} %bitcast.123), calls=%async_computation.1 | async-start | bytes 8388608 | tf_op jit(solution)/shard_map/all_to_all | solution.py:98
  143.0 3.6 copy-start.8
  143.1 19.7 %copy-start.2 = (bf16[128,4096]{1,0:T(8,128)(2,1)S(1)}, bf16[128,4096]{1,0:T(8,128)(2,1)}, u32[]{:S(2)}) copy-start(bf16[128,4096]{1,0:T(8,128)(2,1)} %param.12) | copy-start | bytes 3145732
  158.5 11.5 %all-to-all-start.2 = ((f32[16,1,1024]{2,1,0:T(1,128)}), f32[16,1,1024]{2,1,0:T(1,128)S(1)}, u32[]{:S(2)}, u32[]{:S(2)}) async-start(f32[16,1,1024]{2,1,0:T(1,128)} %reshape.173), calls=%async_computation.2 | async-start | bytes 131072 | tf_op jit(solution)/shard_map/all_to_all | solution.py:135
  162.3 181.3 %reduce-scatter.2.cloned.1.call-start = ((), (), s32[]{:S(2)}) async-start(), calls=%async_computation.5 | async-start | bytes 22282240 | tf_op jit(solution)/shard_map/reduce_scatter | solution.py:179
  189.5 1.0 copy-start.7
  200.1 1.2 copy-start.3
  212.9 0.9 copy-start.5
  212.9 202.5 %all-reduce.3.cloned.1.call-start = ((), (), s32[]{:S(2)}) async-start(), calls=%async_computation.6 | async-start | bytes 2621440 | tf_op jit(solution)/shard_map/psum | solution.py:191
  407.9 11.4 %copy-start.1 = (bf16[256,4096]{1,0:T(8,128)(2,1)S(1)}, bf16[256,4096]{1,0:T(8,128)(2,1)}, u32[]{:S(2)}) copy-start(bf16[256,4096]{1,0:T(8,128)(2,1)} %param.16) | copy-start | bytes 6291460
Sparse Core Ops, SparseCore 0:
  213.0 130.5 reduce-scatter.1
  345.9 66.7 all-reduce.2
where the time goes:
time: 428 us; the launch traced here: 426 us
  waiting for transfers between devices  184 us (43%)
  blocking collectives  64.3 us (15%)
  other arithmetic  54.8 us (13%)
  local copies, waits for them, and re-layouts  46.2 us (11%)
  matrix products  39.1 us (9%)
  starting transfers between devices  23 us (5%)
  between operations  14.3 us (3%)
    reduce_scatter x1, waiting for transfers between devices, on_device(): lax.psum_scatter(grad_term(input_blocks, grad_blocks, query_grad, query_b...  124 us
    psum x1, blocking collectives, on_device(): local_sum, table_sum = lax.psum((local, table_part), 'rep')  64.3 us
    all_to_all x1, waiting for transfers between devices, on_device(): lax.all_to_all(payload.reshape(shards, capacity, model_width), 'tab', spl...  49.6 us
    reduce_sum x2, other arithmetic, place_block(): return jnp.sum(jnp.where(equal, block_spread[:, :, :, None], 0.0), axis=2)  16.5 us
    unnamed x32, local copies, waits for them, and re-layouts  11.1 us
    reduce_sum x2, other arithmetic, pick_block(): return jnp.sum(jnp.where(equal, block_scores[:, :, None, :], 0.0), axis=3)  11.1 us
    reduce_sum x1, other arithmetic, on_device(): jnp.sum(jnp.where(matches, arrived_weights[:, :, None].astype(jnp.float32...  10.9 us
    concatenate x1, other arithmetic, grad_term(): joined = jnp.concatenate([weight_part, key_part], axis=1)  9.21 us
  transfers between devices with their start and end apart: 6, of which 4 were waited for; matrix products, arithmetic and copies ran while one was open for 8% of the time, Pallas kernels for 0%

commit v1 on v0

--- a/solution.py
+++ b/solution.py
@@ -132,13 +132,20 @@
     table_part = lax.dot_general(
         spread_table, arrived, (((0,), (0,)), ((), ())), preferred_element_type=jnp.float32
     )
-    returned = lax.all_to_all(
-        slot_back.reshape(shards, capacity, top_count),
-        "tab",
-        split_axis=0,
-        concat_axis=0,
-        tiled=True,
-    )
+    array = slot_back.reshape(shards, capacity, top_count)
+    ways, here = (lax.axis_size("tab"), lax.axis_index("tab"))
+    width_2 = array.shape[0] // ways
+    dims = list(array.shape)
+    dims[0] = width_2
+    height = dims[0]
+    dims[0] = height * ways
+    full = jnp.zeros(dims, array.dtype)
+    for mask in range(ways):
+        part = lax.dynamic_slice_in_dim(array, (here ^ mask) * width_2, width_2, axis=0)
+        if mask:
+            part = lax.ppermute(part, "tab", [(d, d ^ mask) for d in range(ways)])
+        full = lax.dynamic_update_slice_in_dim(full, part, (here ^ mask) * height, axis=0)
+    returned = full
     slot_grad = lax.dot_general(
         dispatch_wide,
         returned.reshape(slots, top_count),

time: 428 us -> 450 us (1.051)
  starting transfers between devices: 23 us -> 50.4 us
  waiting for transfers between devices: 184 us -> 179 us
    ppermute x0 -> x15, starting transfers between devices: none -> 31.4 us  [on_device(): part = lax.ppermute(part, 'tab', [(d, d ^ mask) for d in range(ways)])]
    all_to_all x1 -> x0, waiting for transfers between devices: 5.8 us -> none  [on_device(): lax.all_to_all(slot_back.reshape(shards, capacity, top_count), 'tab', spl...]
    unnamed x32 -> x30, local copies, waits for them, and re-layouts: 11.1 us -> 10.2 us
  transfers between devices with their start and end apart: 6 -> 20, of which waited for: 4 -> 3; matrix products, arithmetic and copies ran while one was open for 8% -> 8% of each run, Pallas kernels for 0% -> 0%
where the time goes in v1:
time: 450 us; the launch traced here: 449 us
  waiting for transfers between devices  179 us (40%)
  blocking collectives  64.3 us (14%)
  other arithmetic  53.8 us (12%)
  starting transfers between devices  50.4 us (11%)
  local copies, waits for them, and re-layouts  47.1 us (10%)
  matrix products  39.1 us (9%)
  between operations  14.6 us (3%)
    reduce_scatter x1, waiting for transfers between devices, on_device(): lax.psum_scatter(grad_term(input_blocks, grad_blocks, query_grad, query_b...  125 us
    psum x1, blocking collectives, on_device(): local_sum, table_sum = lax.psum((local, table_part), 'rep')  64.3 us
    all_to_all x1, waiting for transfers between devices, on_device(): lax.all_to_all(payload.reshape(shards, capacity, model_width), 'tab', spl...  49.5 us
    ppermute x15, starting transfers between devices, on_device(): part = lax.ppermute(part, 'tab', [(d, d ^ mask) for d in range(ways)])  31.4 us
    reduce_sum x2, other arithmetic, place_block(): return jnp.sum(jnp.where(equal, block_spread[:, :, :, None], 0.0), axis=2)  16.5 us
    reduce_sum x2, other arithmetic, pick_block(): return jnp.sum(jnp.where(equal, block_scores[:, :, None, :], 0.0), axis=3)  11.1 us
    reduce_sum x1, other arithmetic, on_device(): jnp.sum(jnp.where(matches, arrived_weights[:, :, None].astype(jnp.float32...  10.9 us
    unnamed x30, local copies, waits for them, and re-layouts  10.2 us
  transfers between devices with their start and end apart: 20, of which 3 were waited for; matrix products, arithmetic and copies ran while one was open for 8% of the time, Pallas kernels for 0%

profile of v1, /device:TPU:0, one launch (start us, length us, event | category | flops | bytes accessed | tf_op | source)
XLA Modules:
  0.0 448.9 jit_solution(17727805236221014533)
XLA Ops:
  8.4 5.8 %fusion.36 = (bf16[128,1024]{1,0:T(8,128)(2,1)}, f32[128,1024]{1,0:T(8,128)S(1)}) fusion(bf16[128,4096]{1,0:T(8,128)(2,1)} %param.12, bf16[4096,1024]{1,0:T(8,128)(2,1)} %param.14), kind=kOutput, calls=%fused_computation.78 | convolution fusion | flops 1073872896 | bytes 10223616 | tf_op jit(solution)/shard_map/dot_general | solution.py:43
  17.7 16.5 %while.22 = (s32[]{:T(128)}, f32[2,64,4,32]{3,2,1,0:T(4,128)}, s32[2,64,4,32]{3,2,1,0:T(4,128)S(1)}, f32[2,64,4,1024]{3,1,0,2:T(8,128)}, s32[]{:T(128)}) while((s32[]{:T(128)}, f32[2,64,4,32]{3,2,1,0:T(4,128)}, s32[2,64,4,32]{3,2,1,0:T(4,128)S(1)}, f32[2,64,4,1024]{3,1,0,2:T(8,128)}, s32[]{:T(128)}) %tuple.77), condition=%wide.region_2.3_spmd.clone, body=%wide.region_0.2_spmd.clone.sunk | while | flops 25157632 | bytes 5538373 | solution.py:61
  19.7 5.5 %select_reduce_fusion.6 = f32[64,4,32]{2,1,0:T(4,128)S(1)} fusion(f32[64,4,1024]{2,1,0:T(4,128)S(1)} %bitcast.119, s32[64,4,32]{2,1,0:T(4,128)S(1)} %dynamic-slice_bitcast_fusion.6), kind=kLoop, calls=%fused_computation.3.clone.1 | loop fusion | flops 25157632 | bytes 1114112 | tf_op jit(solution)/shard_map/while/body/eval_jaxpr/reduce_sum | solution.py:59
  27.9 5.5 %select_reduce_fusion.6 = f32[64,4,32]{2,1,0:T(4,128)S(1)} fusion(f32[64,4,1024]{2,1,0:T(4,128)S(1)} %bitcast.119, s32[64,4,32]{2,1,0:T(4,128)S(1)} %dynamic-slice_bitcast_fusion.6), kind=kLoop, calls=%fused_computation.3.clone.1 | loop fusion | flops 25157632 | bytes 1114112 | tf_op jit(solution)/shard_map/while/body/eval_jaxpr/reduce_sum | solution.py:59
  48.9 7.1 %all-to-all-start.2 = ((bf16[16,2,512]{2,1,0:T(2,128)(2,1)}), bf16[16,2,512]{2,1,0:T(2,128)(2,1)S(1)}, u32[]{:S(2)}, u32[]{:S(2)}) async-start(bf16[16,2,512]{2,1,0:T(2,128)(2,1)} %reshape.169), calls=%async_computation.3 | async-start | bytes 65536 | tf_op jit(solution)/shard_map/all_to_all | solution.py:112
  69.8 7.3 %all-to-all-start = ((s32[16,1,1024]{2,1,0:T(1,128)}), s32[16,1,1024]{2,1,0:T(1,128)}, u32[]{:S(2)}, u32[]{:S(2)}) async-start(s32[16,1,1024]{2,1,0:T(1,128)} %reshape.171), calls=%async_computation | async-start | bytes 131072 | tf_op jit(solution)/shard_map/all_to_all | solution.py:105
  80.3 4.5 %all-to-all-done = s32[16,1,1024]{2,1,0:T(1,128)} async-done(((s32[16,1,1024]{2,1,0:T(1,128)}), s32[16,1,1024]{2,1,0:T(1,128)}, u32[]{:S(2)}, u32[]{:S(2)}) %all-to-all-start) | async-done | bytes 65568 | tf_op jit(solution)/shard_map/all_to_all | solution.py:105
  84.8 4.5 %all-to-all-start.1 = ((bf16[16,32,4096]{2,1,0:T(8,128)(2,1)}), bf16[16,32,4096]{2,1,0:T(8,128)(2,1)}, u32[]{:S(2)}, u32[]{:S(2)}) async-start(bf16[16,32,4096]{2,1,0:T(8,128)(2,1)} %bitcast.121), calls=%async_computation.1 | async-start | bytes 8388608 | tf_op jit(solution)/shard_map/all_to_all | solution.py:98
  93.6 49.5 %all-to-all-done.1 = bf16[16,32,4096]{2,1,0:T(8,128)(2,1)} async-done(((bf16[16,32,4096]{2,1,0:T(8,128)(2,1)}), bf16[16,32,4096]{2,1,0:T(8,128)(2,1)}, u32[]{:S(2)}, u32[]{:S(2)}) %all-to-all-start.1) | async-done | bytes 4194336 | tf_op jit(solution)/shard_map/all_to_all | solution.py:98
  143.1 3.6 fusion.37
  146.7 10.9 %select_reduce_fusion.2 = (bf16[512,256]{1,0:T(8,128)(2,1)}, f32[512,32]{1,0:T(8,128)S(1)}) fusion(f32[512,32]{1,0:T(8,128)} %bitcast.139, s32[512,32]{1,0:T(8,128)S(1)} %bitcast.140, f32[512,256]{1,0:T(8,128)S(1)} %fusion.37), kind=kLoop, calls=%fused_computation.14 | loop fusion | flops 20824064 | bytes 983040 | tf_op jit(solution)/shard_map/reduce_sum | solution.py:129
  165.0 4.5 collective-permute-start.6
  170.7 5.2 %collective-permute-start.9 = (f32[1,32,32]{2,1,0:T(8,128)S(1)}, f32[1,32,32]{2,1,0:T(8,128)S(1)}, u32[]{:S(2)}, u32[]{:S(2)}) collective-permute-start(f32[1,32,32]{2,1,0:T(8,128)S(1)} %get-tuple-element.125), channel_id=1, source_target_pairs={{0,10},{1,11},{2,8},{3,9},{4,14},{5,15},{6,12},{7,13},{8,2},{9,3},... | collective-permute-start | bytes 12296 | tf_op jit(solution)/shard_map/ppermute | solution.py:146
  175.9 3.6 collective-permute-start.10
  179.7 4.6 %collective-permute-start.13 = (f32[1,32,32]{2,1,0:T(8,128)S(1)}, f32[1,32,32]{2,1,0:T(8,128)S(1)}, u32[]{:S(2)}, u32[]{:S(2)}) collective-permute-start(f32[1,32,32]{2,1,0:T(8,128)S(1)} %get-tuple-element.121), channel_id=1, source_target_pairs={{0,14},{1,15},{2,12},{3,13},{4,10},{5,11},{6,8},{7,9},{8,6},{9,7},... | collective-permute-start | bytes 12296 | tf_op jit(solution)/shard_map/ppermute | solution.py:146
  184.3 4.8 %collective-permute-start.14 = (f32[1,32,32]{2,1,0:T(8,128)S(1)}, f32[1,32,32]{2,1,0:T(8,128)S(1)}, u32[]{:S(2)}, u32[]{:S(2)}) collective-permute-start(f32[1,32,32]{2,1,0:T(8,128)S(1)} %get-tuple-element.120), channel_id=1, source_target_pairs={{0,15},{1,14},{2,13},{3,12},{4,11},{5,10},{6,9},{7,8},{8,7},{9,6},... | collective-permute-start | bytes 12296 | tf_op jit(solution)/shard_map/ppermute | solution.py:146
  194.2 17.1 %while.23 = (s32[]{:T(128)}, bf16[2,64,4,1024]{3,2,1,0:T(4,128)(2,1)S(1)}, s32[2,64,4,32]{3,2,1,0:T(4,128)S(1)}, f32[2,64,4,32]{3,2,1,0:T(4,128)S(1)}, s32[]{:T(128)}) while((s32[]{:T(128)}, bf16[2,64,4,1024]{3,2,1,0:T(4,128)(2,1)S(1)}, s32[2,64,4,32]{3,2,1,0:T(4,128)S(1)}, f32[2,64,4,32]{3,2,1,0:T(4,128)S(1)}, s32[]{:T(128)}) %tuple.79), condition=%wide.region_11.12_spmd.clone, body=%wide.region_9.11_spmd.clone.sunk | while | flops 24903680 | bytes 1769545 | solution.py:165
  194.3 8.3 %select_reduce_fusion.7 = bf16[64,4,1024]{2,1,0:T(4,128)(2,1)S(1)} fusion(f32[64,4,32]{2,1,0:T(4,128)S(1)} %dynamic-slice_bitcast_fusion.7, s32[64,4,32]{2,1,0:T(4,128)S(1)} %dynamic-slice_bitcast_fusion.8), kind=kLoop, calls=%fused_computation.9.clone.1 | loop fusion | flops 24903680 | bytes 589824 | tf_op jit(solution)/shard_map/while/body/eval_jaxpr/reduce_sum | solution.py:163
  202.9 8.3 %select_reduce_fusion.7 = bf16[64,4,1024]{2,1,0:T(4,128)(2,1)S(1)} fusion(f32[64,4,32]{2,1,0:T(4,128)S(1)} %dynamic-slice_bitcast_fusion.7, s32[64,4,32]{2,1,0:T(4,128)S(1)} %dynamic-slice_bitcast_fusion.8), kind=kLoop, calls=%fused_computation.9.clone.1 | loop fusion | flops 24903680 | bytes 589824 | tf_op jit(solution)/shard_map/while/body/eval_jaxpr/reduce_sum | solution.py:163
  225.6 9.0 %pad_maximum_fusion = f32[16,320,1024]{2,1,0:T(8,128)} fusion(f32[16,64,1024]{2,1,0:T(8,128)S(1)} %bitcast.123, f32[16,256,1024]{2,1,0:T(8,128)S(1)} %convolution_bitcast_fusion), kind=kLoop, calls=%fused_computation.13 | loop fusion | flops 5242880 | bytes 41943040 | tf_op jit(solution)/shard_map/concatenate | solution.py:22
  235.6 5.4 %fusion.38 = f32[256,4096]{1,0:T(8,128)} fusion(bf16[512,256]{1,0:T(8,128)(2,1)S(1)} %copy-done.5, bf16[512,4096]{1,0:T(8,128)(2,1)} %bitcast.9), kind=kOutput, calls=%fused_computation.82 | convolution fusion | flops 1073741824 | bytes 8650752 | tf_op jit(solution)/shard_map/dot_general | solution.py:132
  241.0 125.3 %reduce-scatter.2.cloned.1.call-done = f32[320,1024]{1,0:T(8,128)} async-done(((f32[5120,1024]{1,0:T(8,128)}), f32[320,1024]{1,0:T(8,128)}) %reduce-scatter.2.cloned.1.call-update) | async-done | bytes 1310736 | tf_op jit(solution)/shard_map/reduce_scatter | solution.py:186
  366.3 64.3 %all-reduce.4 = bf16[256,4096]{1,0:T(8,128)(2,1)} all-reduce(f32[256,4096]{1,0:T(8,128)} %fusion.38), channel_id=1, replica_groups=mesh['rep'=8,'tab'=16] {'rep'}, use_global_device_ids=true, to_apply=%region_15.16 | all-reduce | flops 1048576 | bytes 6291456 | tf_op jit(solution)/shard_map/psum | solution.py:198
  430.6 7.4 %convolution_convert_fusion.1 = bf16[128,4096]{1,0:T(8,128)(2,1)} fusion(bf16[128,1024]{0,1:T(8,128)(2,1)S(1)} %bitcast.130, bf16[4096,1024]{1,0:T(8,128)(2,1)} %param.14), kind=kOutput, calls=%fused_computation.19 | convolution fusion | flops 1074266112 | bytes 9699328 | tf_op jit(solution)/shard_map/dot_general | solution.py:178
  (158 shorter events, 79.1 us)
Async XLA Ops:
  7.2 135.9 %copy-start = (bf16[256,4096]{1,0:T(8,128)(2,1)S(1)}, bf16[256,4096]{1,0:T(8,128)(2,1)}, u32[]{:S(2)}) copy-start(bf16[256,4096]{1,0:T(8,128)(2,1)} %param.16) | copy-start | bytes 6291460
  17.7 24.9 %copy-start.10 = (s32[128,2,1]{0,2,1:T(1,128)S(1)}, s32[128,2,1]{0,2,1:T(1,128)}, u32[]{:S(2)}) copy-start(s32[128,2,1]{0,2,1:T(1,128)} %param.17) | copy-start | bytes 3076
  34.2 42.9 %copy-start.6 = (bf16[128,4096]{1,0:T(8,128)(2,1)S(1)}, bf16[128,4096]{1,0:T(8,128)(2,1)}, u32[]{:S(2)}) copy-start(bf16[128,4096]{1,0:T(8,128)(2,1)} %param.13) | copy-start | bytes 3145732
  48.9 21.0 %all-to-all-start.2 = ((bf16[16,2,512]{2,1,0:T(2,128)(2,1)}), bf16[16,2,512]{2,1,0:T(2,128)(2,1)S(1)}, u32[]{:S(2)}, u32[]{:S(2)}) async-start(bf16[16,2,512]{2,1,0:T(2,128)(2,1)} %reshape.169), calls=%async_computation.3 | async-start | bytes 65536 | tf_op jit(solution)/shard_map/all_to_all | solution.py:112
  69.8 15.0 %all-to-all-start = ((s32[16,1,1024]{2,1,0:T(1,128)}), s32[16,1,1024]{2,1,0:T(1,128)}, u32[]{:S(2)}, u32[]{:S(2)}) async-start(s32[16,1,1024]{2,1,0:T(1,128)} %reshape.171), calls=%async_computation | async-start | bytes 131072 | tf_op jit(solution)/shard_map/all_to_all | solution.py:105
  84.8 58.3 %all-to-all-start.1 = ((bf16[16,32,4096]{2,1,0:T(8,128)(2,1)}), bf16[16,32,4096]{2,1,0:T(8,128)(2,1)}, u32[]{:S(2)}, u32[]{:S(2)}) async-start(bf16[16,32,4096]{2,1,0:T(8,128)(2,1)} %bitcast.121), calls=%async_computation.1 | async-start | bytes 8388608 | tf_op jit(solution)/shard_map/all_to_all | solution.py:98
  89.4 276.9 %reduce-scatter.2.cloned.1.call-start = ((), (), s32[]{:S(2)}) async-start(), calls=%async_computation.4 | async-start | bytes 22282240 | tf_op jit(solution)/shard_map/reduce_scatter | solution.py:186
  143.1 46.1 %copy-start.2 = (bf16[128,4096]{1,0:T(8,128)(2,1)S(1)}, bf16[128,4096]{1,0:T(8,128)(2,1)}, u32[]{:S(2)}) copy-start(bf16[128,4096]{1,0:T(8,128)(2,1)} %param.12) | copy-start | bytes 3145732
  157.6 5.6 %collective-permute-start = (f32[1,32,32]{2,1,0:T(8,128)S(1)}, f32[1,32,32]{2,1,0:T(8,128)S(1)}, u32[]{:S(2)}, u32[]{:S(2)}) collective-permute-start(f32[1,32,32]{2,1,0:T(8,128)S(1)} %get-tuple-element.134), channel_id=1, source_target_pairs={{0,1},{1,0},{2,3},{3,2},{4,5},{5,4},{6,7},{7,6},{8,9},{9,8},{10,11... | collective-permute-start | bytes 12296 | tf_op jit(solution)/shard_map/ppermute | solution.py:146
  158.3 6.7 %collective-permute-start.1 = (f32[1,32,32]{2,1,0:T(8,128)S(1)}, f32[1,32,32]{2,1,0:T(8,128)S(1)}, u32[]{:S(2)}, u32[]{:S(2)}) collective-permute-start(f32[1,32,32]{2,1,0:T(8,128)S(1)} %get-tuple-element.133), channel_id=1, source_target_pairs={{0,2},{1,3},{2,0},{3,1},{4,6},{5,7},{6,4},{7,5},{8,10},{9,11},{10,... | collective-permute-start | bytes 12296 | tf_op jit(solution)/shard_map/ppermute | solution.py:146
  159.4 10.1 %collective-permute-start.2 = (f32[1,32,32]{2,1,0:T(8,128)S(1)}, f32[1,32,32]{2,1,0:T(8,128)S(1)}, u32[]{:S(2)}, u32[]{:S(2)}) collective-permute-start(f32[1,32,32]{2,1,0:T(8,128)S(1)} %get-tuple-element.132), channel_id=1, source_target_pairs={{0,3},{1,2},{2,1},{3,0},{4,7},{5,6},{6,5},{7,4},{8,11},{9,10},{10,... | collective-permute-start | bytes 12296 | tf_op jit(solution)/shard_map/ppermute | solution.py:146
  162.4 8.3 %collective-permute-start.3 = (f32[1,32,32]{2,1,0:T(8,128)S(1)}, f32[1,32,32]{2,1,0:T(8,128)S(1)}, u32[]{:S(2)}, u32[]{:S(2)}) collective-permute-start(f32[1,32,32]{2,1,0:T(8,128)S(1)} %get-tuple-element.131), channel_id=1, source_target_pairs={{0,4},{1,5},{2,6},{3,7},{4,0},{5,1},{6,2},{7,3},{8,12},{9,13},{10,... | collective-permute-start | bytes 12296 | tf_op jit(solution)/shard_map/ppermute | solution.py:146
  162.4 8.3 %collective-permute-start.4 = (f32[1,32,32]{2,1,0:T(8,128)S(1)}, f32[1,32,32]{2,1,0:T(8,128)S(1)}, u32[]{:S(2)}, u32[]{:S(2)}) collective-permute-start(f32[1,32,32]{2,1,0:T(8,128)S(1)} %get-tuple-element.130), channel_id=1, source_target_pairs={{0,5},{1,4},{2,7},{3,6},{4,1},{5,0},{6,3},{7,2},{8,13},{9,12},{10,... | collective-permute-start | bytes 12296 | tf_op jit(solution)/shard_map/ppermute | solution.py:146
  163.2 12.7 %collective-permute-start.5 = (f32[1,32,32]{2,1,0:T(8,128)S(1)}, f32[1,32,32]{2,1,0:T(8,128)S(1)}, u32[]{:S(2)}, u32[]{:S(2)}) collective-permute-start(f32[1,32,32]{2,1,0:T(8,128)S(1)} %get-tuple-element.129), channel_id=1, source_target_pairs={{0,6},{1,7},{2,4},{3,5},{4,2},{5,3},{6,0},{7,1},{8,14},{9,15},{10,... | collective-permute-start | bytes 12296 | tf_op jit(solution)/shard_map/ppermute | solution.py:146
  165.0 14.5 %collective-permute-start.6 = (f32[1,32,32]{2,1,0:T(8,128)S(1)}, f32[1,32,32]{2,1,0:T(8,128)S(1)}, u32[]{:S(2)}, u32[]{:S(2)}) collective-permute-start(f32[1,32,32]{2,1,0:T(8,128)S(1)} %get-tuple-element.128), channel_id=1, source_target_pairs={{0,7},{1,6},{2,5},{3,4},{4,3},{5,2},{6,1},{7,0},{8,15},{9,14},{10,... | collective-permute-start | bytes 12296 | tf_op jit(solution)/shard_map/ppermute | solution.py:146
  169.5 10.1 %collective-permute-start.7 = (f32[1,32,32]{2,1,0:T(8,128)S(1)}, f32[1,32,32]{2,1,0:T(8,128)S(1)}, u32[]{:S(2)}, u32[]{:S(2)}) collective-permute-start(f32[1,32,32]{2,1,0:T(8,128)S(1)} %get-tuple-element.127), channel_id=1, source_target_pairs={{0,8},{1,9},{2,10},{3,11},{4,12},{5,13},{6,14},{7,15},{8,0},{9,1},... | collective-permute-start | bytes 12296 | tf_op jit(solution)/shard_map/ppermute | solution.py:146
  170.7 8.9 %collective-permute-start.8 = (f32[1,32,32]{2,1,0:T(8,128)S(1)}, f32[1,32,32]{2,1,0:T(8,128)S(1)}, u32[]{:S(2)}, u32[]{:S(2)}) collective-permute-start(f32[1,32,32]{2,1,0:T(8,128)S(1)} %get-tuple-element.126), channel_id=1, source_target_pairs={{0,9},{1,8},{2,11},{3,10},{4,13},{5,12},{6,15},{7,14},{8,1},{9,0},... | collective-permute-start | bytes 12296 | tf_op jit(solution)/shard_map/ppermute | solution.py:146
  170.7 13.5 %collective-permute-start.9 = (f32[1,32,32]{2,1,0:T(8,128)S(1)}, f32[1,32,32]{2,1,0:T(8,128)S(1)}, u32[]{:S(2)}, u32[]{:S(2)}) collective-permute-start(f32[1,32,32]{2,1,0:T(8,128)S(1)} %get-tuple-element.125), channel_id=1, source_target_pairs={{0,10},{1,11},{2,8},{3,9},{4,14},{5,15},{6,12},{7,13},{8,2},{9,3},... | collective-permute-start | bytes 12296 | tf_op jit(solution)/shard_map/ppermute | solution.py:146
  175.9 16.5 %collective-permute-start.10 = (f32[1,32,32]{2,1,0:T(8,128)S(1)}, f32[1,32,32]{2,1,0:T(8,128)S(1)}, u32[]{:S(2)}, u32[]{:S(2)}) collective-permute-start(f32[1,32,32]{2,1,0:T(8,128)S(1)} %get-tuple-element.124), channel_id=1, source_target_pairs={{0,11},{1,10},{2,9},{3,8},{4,15},{5,14},{6,13},{7,12},{8,3},{9,2},... | collective-permute-start | bytes 12296 | tf_op jit(solution)/shard_map/ppermute | solution.py:146
  179.6 13.1 %collective-permute-start.11 = (f32[1,32,32]{2,1,0:T(8,128)S(1)}, f32[1,32,32]{2,1,0:T(8,128)S(1)}, u32[]{:S(2)}, u32[]{:S(2)}) collective-permute-start(f32[1,32,32]{2,1,0:T(8,128)S(1)} %get-tuple-element.123), channel_id=1, source_target_pairs={{0,12},{1,13},{2,14},{3,15},{4,8},{5,9},{6,10},{7,11},{8,4},{9,5},... | collective-permute-start | bytes 12296 | tf_op jit(solution)/shard_map/ppermute | solution.py:146
  179.6 13.2 %collective-permute-start.12 = (f32[1,32,32]{2,1,0:T(8,128)S(1)}, f32[1,32,32]{2,1,0:T(8,128)S(1)}, u32[]{:S(2)}, u32[]{:S(2)}) collective-permute-start(f32[1,32,32]{2,1,0:T(8,128)S(1)} %get-tuple-element.122), channel_id=1, source_target_pairs={{0,13},{1,12},{2,15},{3,14},{4,9},{5,8},{6,11},{7,10},{8,5},{9,4},... | collective-permute-start | bytes 12296 | tf_op jit(solution)/shard_map/ppermute | solution.py:146
  179.7 13.3 %collective-permute-start.13 = (f32[1,32,32]{2,1,0:T(8,128)S(1)}, f32[1,32,32]{2,1,0:T(8,128)S(1)}, u32[]{:S(2)}, u32[]{:S(2)}) collective-permute-start(f32[1,32,32]{2,1,0:T(8,128)S(1)} %get-tuple-element.121), channel_id=1, source_target_pairs={{0,14},{1,15},{2,12},{3,13},{4,10},{5,11},{6,8},{7,9},{8,6},{9,7},... | collective-permute-start | bytes 12296 | tf_op jit(solution)/shard_map/ppermute | solution.py:146
  184.3 8.8 %collective-permute-start.14 = (f32[1,32,32]{2,1,0:T(8,128)S(1)}, f32[1,32,32]{2,1,0:T(8,128)S(1)}, u32[]{:S(2)}, u32[]{:S(2)}) collective-permute-start(f32[1,32,32]{2,1,0:T(8,128)S(1)} %get-tuple-element.120), channel_id=1, source_target_pairs={{0,15},{1,14},{2,13},{3,12},{4,11},{5,10},{6,9},{7,8},{8,7},{9,6},... | collective-permute-start | bytes 12296 | tf_op jit(solution)/shard_map/ppermute | solution.py:146
  234.6 203.4 %all-reduce.3.cloned.1.call-start = ((), (), s32[]{:S(2)}) async-start(), calls=%async_computation.5 | async-start | bytes 2621440 | tf_op jit(solution)/shard_map/psum | solution.py:198
  (7 other events, 24.5 us)
Sparse Core Ops, SparseCore 0:
  234.8 131.4 reduce-scatter.1
  368.7 66.7 all-reduce.2
